TPU v7x, 32 devices: a whole 2x2x4 slice. The times are simulated.
32 devices in a mesh: fsdp: 4 (over y, x), context: 4 (over z), tensor: 2 (over core).
Axes of the slice: x: 2, y: 2, z: 4, core: 2. Of those that a mesh axis runs over, the one named last changes fastest.
Arguments:
- layer_input: bfloat16 [4, 1024, 2048], P('fsdp', 'context'), may hold values from -6 to 6
- prefix: int32 [4], P('fsdp'), may hold values from 102 to 512
- attn_gain: float32 [2048], P(('fsdp', 'context')), may hold values from 0.1 to 1.9
- q_weight: float32 [2048, 2048], P(('fsdp', 'context'), 'tensor'), may hold values from -0.125 to 0.125
- k_weight: float32 [2048, 512], P(('fsdp', 'context'), 'tensor'), may hold values from -0.125 to 0.125
- v_weight: float32 [2048, 512], P(('fsdp', 'context'), 'tensor'), may hold values from -0.125 to 0.125
- output_weight: float32 [2048, 2048], P(('fsdp', 'context'), 'tensor'), may hold values from -0.75 to 0.75
- mlp_gain: float32 [2048], P(('fsdp', 'context')), may hold values from 0.1 to 1.9
- gate_weight: float32 [2048, 8192], P(('fsdp', 'context'), 'tensor'), may hold values from -0.125 to 0.125
- up_weight: float32 [2048, 8192], P(('fsdp', 'context'), 'tensor'), may hold values from -0.125 to 0.125
- down_weight: float32 [2048, 8192], P(('fsdp', 'context'), 'tensor'), may hold values from -0.0625 to 0.0625
- cotangent: bfloat16 [4, 1024, 2048], P('fsdp', 'context'), may hold values from -6 to 6
Outputs:
- layer_output: bfloat16 [4, 1024, 2048], P('fsdp', 'context')
- input_grad: bfloat16 [4, 1024, 2048], P('fsdp', 'context')
- attn_gain_grad: float32 [2048], P(('fsdp', 'context'))
- q_weight_grad: float32 [2048, 2048], P(('fsdp', 'context'), 'tensor')
- k_weight_grad: float32 [2048, 512], P(('fsdp', 'context'), 'tensor')
- v_weight_grad: float32 [2048, 512], P(('fsdp', 'context'), 'tensor')
- o_weight_grad: float32 [2048, 2048], P(('fsdp', 'context'), 'tensor')
- mlp_gain_grad: float32 [2048], P(('fsdp', 'context'))
- gate_weight_grad: float32 [2048, 8192], P(('fsdp', 'context'), 'tensor')
- up_weight_grad: float32 [2048, 8192], P(('fsdp', 'context'), 'tensor')
- down_weight_grad: float32 [2048, 8192], P(('fsdp', 'context'), 'tensor')
Inputs may be any that keep to these rules, and one draw needn't show every extreme that they name: prefix counts whole leading tokens of a sequence of 1024.
All inputs are finite; a program needn't handle non-finite values.
Results may differ from a plain program's by a relative error of at most 0.019.
Values may be sent and summed in bfloat16 or wider, within the bound.
No kernel may reach another device: no remote copies, remote signals or barrier semaphores. Data moves between devices by JAX's collectives and lax.ppermute only.
A program may use at most 384 MiB of HBM per device.

v0:
```python
from functools import partial
import math
import jax
import jax.numpy as jnp
from jax import lax
from jax.sharding import PartitionSpec as P

HEADS = 32
KV_HEADS = 8
HEAD_DIM = 64
EPS = 1e-05


def rope_tables(length, head_dim):
    half_dim = head_dim // 2
    freq_index = jnp.arange(half_dim, dtype=jnp.float32)
    base_freq = 1.0 / jnp.power(500000.0, 2.0 * freq_index / head_dim)
    wave_len = 2.0 * math.pi / base_freq
    mix_ratio = jnp.clip((8192.0 / wave_len - 1.0) / 3.0, 0.0, 1.0)
    scaled = (1.0 - mix_ratio) * base_freq / 32.0 + mix_ratio * base_freq
    position = jnp.arange(length, dtype=jnp.float32)
    angles = position[:, None] * scaled[None, :]
    angles = jnp.concatenate([angles, angles], axis=1)
    return (jnp.cos(angles), jnp.sin(angles))


def rotate(tensor_in, cos_table, sin_table):
    half_dim = tensor_in.shape[-1] // 2
    turned = jnp.concatenate([-tensor_in[..., half_dim:], tensor_in[..., :half_dim]], axis=-1)
    return tensor_in * cos_table[:, None, :] + turned * sin_table[:, None, :]


def rotate_rows(flat_in, cos_table, sin_table):
    shaped = flat_in.reshape(flat_in.shape[0], flat_in.shape[1], -1, HEAD_DIM)
    return rotate(shaped, cos_table, sin_table).reshape(flat_in.shape)


def norm_forward(hidden, gain_row):
    inv_rms = lax.rsqrt(jnp.mean(hidden * hidden, axis=-1, keepdims=True) + EPS)
    return ((hidden * inv_rms * gain_row.astype(jnp.float32)).astype(jnp.bfloat16), inv_rms)


def norm_reverse_pass(hidden, inv_rms, gain_row, grad_in):
    weighted = grad_in * gain_row.astype(jnp.float32)
    grad_hidden = inv_rms * weighted - hidden * (inv_rms * inv_rms * inv_rms) * jnp.mean(
        weighted * hidden, axis=-1, keepdims=True
    )
    gain_grad = jnp.sum(grad_in * hidden * inv_rms, axis=(0, 1))
    return (grad_hidden, gain_grad)


def masked_scores(query, keys, prefix_len, first_row):
    row_count = query.shape[0]
    key_count = keys.shape[0]
    kv_local = keys.shape[1] // HEAD_DIM
    grouped = query.reshape(row_count, kv_local, HEADS // KV_HEADS, HEAD_DIM)
    key_heads = keys.reshape(key_count, kv_local, HEAD_DIM)
    logits = jnp.einsum(
        "ikgd,jkd->kgij", grouped, key_heads, preferred_element_type=jnp.float32
    ) * HEAD_DIM ** (-0.5)
    query_pos = first_row + jnp.arange(row_count, dtype=jnp.int32)
    key_pos = jnp.arange(key_count, dtype=jnp.int32)
    allowed = (key_pos[None, :] <= query_pos[:, None]) | (key_pos[None, :] < prefix_len)
    return (jnp.where(allowed, logits, -1e30), grouped, key_heads)


def attend_forward(operands, first_row):
    query, keys, values, prefix_len = operands
    logits, grouped, key_heads = masked_scores(query, keys, prefix_len, first_row)
    row_max = jnp.max(logits, axis=-1, keepdims=True)
    exp_scores = jnp.exp(logits - row_max)
    row_total = jnp.sum(exp_scores, axis=-1, keepdims=True)
    probs_low = (exp_scores / row_total).astype(jnp.bfloat16)
    value_heads = values.reshape(key_heads.shape)
    mixed_out = jnp.einsum(
        "kgij,jkd->ikgd", probs_low, value_heads, preferred_element_type=jnp.float32
    )
    log_total = (row_max + jnp.log(row_total))[..., 0]
    return (mixed_out.reshape(query.shape[0], -1), log_total)


def attend_backward(operands, first_row):
    query, keys, values, prefix_len, log_total, grad_out = operands
    logits, grouped, key_heads = masked_scores(query, keys, prefix_len, first_row)
    probs = jnp.exp(logits - log_total[..., None])
    value_heads = values.reshape(key_heads.shape)
    grad_heads = grad_out.reshape(grouped.shape)
    value_grad = jnp.einsum(
        "kgij,ikgd->jkd", probs.astype(jnp.bfloat16), grad_heads, preferred_element_type=jnp.float32
    )
    grad_probs = jnp.einsum(
        "ikgd,jkd->kgij", grad_heads, value_heads, preferred_element_type=jnp.float32
    )
    delta_rows = jnp.sum(probs * grad_probs, axis=-1, keepdims=True)
    grad_scores = (probs * (grad_probs - delta_rows)).astype(jnp.bfloat16)
    query_grad = jnp.einsum(
        "kgij,jkd->ikgd", grad_scores, key_heads, preferred_element_type=jnp.float32
    ) * HEAD_DIM ** (-0.5)
    key_grad = jnp.einsum(
        "kgij,ikgd->jkd", grad_scores, grouped, preferred_element_type=jnp.float32
    ) * HEAD_DIM ** (-0.5)
    return (
        query_grad.reshape(query.shape[0], -1),
        key_grad.reshape(keys.shape[0], -1),
        value_grad.reshape(keys.shape[0], -1),
    )


def on_device(
    layer_input,
    prefix,
    attn_gain,
    q_weight,
    k_weight,
    v_weight,
    output_weight,
    mlp_gain,
    gate_weight,
    up_weight,
    down_weight,
    cotangent,
):
    row_count = layer_input.shape[1]
    key_count = row_count * lax.axis_size("context")
    first_row = lax.axis_index("context") * row_count
    cos_all, sin_all = rope_tables(key_count, HEAD_DIM)
    cos_table = lax.dynamic_slice_in_dim(cos_all, first_row, row_count, 0)
    sin_table = lax.dynamic_slice_in_dim(sin_all, first_row, row_count, 0)
    gain_one, q_full, k_full, v_full, o_full = (
        lax.all_gather(attn_gain.astype(jnp.bfloat16), ("fsdp", "context"), axis=0, tiled=True),
        lax.all_gather(q_weight.astype(jnp.bfloat16), ("fsdp", "context"), axis=0, tiled=True),
        lax.all_gather(k_weight.astype(jnp.bfloat16), ("fsdp", "context"), axis=0, tiled=True),
        lax.all_gather(v_weight.astype(jnp.bfloat16), ("fsdp", "context"), axis=0, tiled=True),
        lax.all_gather(output_weight.astype(jnp.bfloat16), ("fsdp", "context"), axis=0, tiled=True),
    )
    hidden_in = layer_input.astype(jnp.float32)
    normed_one, rms_one = norm_forward(hidden_in, gain_one)
    query = jnp.einsum("scd,de->sce", normed_one, q_full, preferred_element_type=jnp.float32)
    key_proj = jnp.einsum("scd,de->sce", normed_one, k_full, preferred_element_type=jnp.float32)
    value_low = jnp.einsum(
        "scd,de->sce", normed_one, v_full, preferred_element_type=jnp.float32
    ).astype(jnp.bfloat16)
    query_rot = rotate_rows(query, cos_table, sin_table).astype(jnp.bfloat16)
    key_rot = rotate_rows(key_proj, cos_table, sin_table).astype(jnp.bfloat16)
    keys_all, values_all = (
        lax.all_gather(key_rot, "context", axis=1, tiled=True),
        lax.all_gather(value_low, "context", axis=1, tiled=True),
    )
    attended, log_total = lax.map(
        partial(attend_forward, first_row=first_row), (query_rot, keys_all, values_all, prefix)
    )
    attended_low = attended.astype(jnp.bfloat16)
    attn_branch = lax.psum(
        jnp.einsum("sce,de->scd", attended_low, o_full, preferred_element_type=jnp.float32),
        "tensor",
    )
    resid = hidden_in + attn_branch
    gain_two, gate_full, up_full, down_full = (
        lax.all_gather(mlp_gain.astype(jnp.bfloat16), ("fsdp", "context"), axis=0, tiled=True),
        lax.all_gather(gate_weight.astype(jnp.bfloat16), ("fsdp", "context"), axis=0, tiled=True),
        lax.all_gather(up_weight.astype(jnp.bfloat16), ("fsdp", "context"), axis=0, tiled=True),
        lax.all_gather(down_weight.astype(jnp.bfloat16), ("fsdp", "context"), axis=0, tiled=True),
    )
    normed_two, rms_two = norm_forward(resid, gain_two)
    gate_proj = jnp.einsum("scd,df->scf", normed_two, gate_full, preferred_element_type=jnp.float32)
    up_projection = jnp.einsum(
        "scd,df->scf", normed_two, up_full, preferred_element_type=jnp.float32
    )
    inner_act = (jax.nn.silu(gate_proj) * up_projection).astype(jnp.bfloat16)
    mlp_branch = lax.psum(
        jnp.einsum("scf,df->scd", inner_act, down_full, preferred_element_type=jnp.float32).astype(
            jnp.bfloat16
        ),
        "tensor",
    ).astype(jnp.float32)
    layer_output = (resid + mlp_branch).astype(jnp.bfloat16)
    gain_two, gate_full, up_full, down_full = (
        lax.all_gather(mlp_gain.astype(jnp.bfloat16), ("fsdp", "context"), axis=0, tiled=True),
        lax.all_gather(gate_weight.astype(jnp.bfloat16), ("fsdp", "context"), axis=0, tiled=True),
        lax.all_gather(up_weight.astype(jnp.bfloat16), ("fsdp", "context"), axis=0, tiled=True),
        lax.all_gather(down_weight.astype(jnp.bfloat16), ("fsdp", "context"), axis=0, tiled=True),
    )
    grad_inner = jnp.einsum("scd,df->scf", cotangent, down_full, preferred_element_type=jnp.float32)
    squash = jax.nn.sigmoid(gate_proj)
    grad_gate = (grad_inner * up_projection * squash * (1.0 + gate_proj * (1.0 - squash))).astype(
        jnp.bfloat16
    )
    grad_up = (grad_inner * gate_proj * squash).astype(jnp.bfloat16)
    grad_normed_two = lax.psum(
        (
            jnp.einsum("scf,df->scd", grad_gate, gate_full, preferred_element_type=jnp.float32)
            + jnp.einsum("scf,df->scd", grad_up, up_full, preferred_element_type=jnp.float32)
        ).astype(jnp.bfloat16),
        "tensor",
    ).astype(jnp.float32)
    resid_part, gain_two_grad = norm_reverse_pass(resid, rms_two, gain_two, grad_normed_two)
    grad_resid = cotangent.astype(jnp.float32) + resid_part
    gate_part = jnp.einsum("scd,scf->df", normed_two, grad_gate, preferred_element_type=jnp.float32)
    up_part = jnp.einsum("scd,scf->df", normed_two, grad_up, preferred_element_type=jnp.float32)
    pair_part = jnp.stack([gate_part, up_part], axis=1)
    down_part = jnp.einsum("scd,scf->df", cotangent, inner_act, preferred_element_type=jnp.float32)
    mlp_grads = lax.psum_scatter(
        jnp.concatenate([pair_part, down_part[:, None, :]], axis=1),
        ("fsdp", "context"),
        scatter_dimension=0,
        tiled=True,
    )
    gate_share = mlp_grads[:, 0, :]
    up_share = mlp_grads[:, 1, :]
    down_share = mlp_grads[:, 2, :]
    gain_one, q_full, k_full, v_full, o_full = (
        lax.all_gather(attn_gain.astype(jnp.bfloat16), ("fsdp", "context"), axis=0, tiled=True),
        lax.all_gather(q_weight.astype(jnp.bfloat16), ("fsdp", "context"), axis=0, tiled=True),
        lax.all_gather(k_weight.astype(jnp.bfloat16), ("fsdp", "context"), axis=0, tiled=True),
        lax.all_gather(v_weight.astype(jnp.bfloat16), ("fsdp", "context"), axis=0, tiled=True),
        lax.all_gather(output_weight.astype(jnp.bfloat16), ("fsdp", "context"), axis=0, tiled=True),
    )
    keys_all, values_all = (
        lax.all_gather(key_rot, "context", axis=1, tiled=True),
        lax.all_gather(value_low, "context", axis=1, tiled=True),
    )
    branch_gradient = grad_resid.astype(jnp.bfloat16)
    o_part = jnp.einsum(
        "scd,sce->de", branch_gradient, attended_low, preferred_element_type=jnp.float32
    )
    grad_att = jnp.einsum(
        "scd,de->sce", branch_gradient, o_full, preferred_element_type=jnp.float32
    ).astype(jnp.bfloat16)
    query_grad, every_key_gradient, value_grad_all = lax.map(
        partial(attend_backward, first_row=first_row),
        (query_rot, keys_all, values_all, prefix, log_total, grad_att),
    )
    key_grad, value_grad = (
        lax.psum_scatter(
            every_key_gradient.astype(jnp.bfloat16), "context", scatter_dimension=1, tiled=True
        ).astype(jnp.float32),
        lax.psum_scatter(
            value_grad_all.astype(jnp.bfloat16), "context", scatter_dimension=1, tiled=True
        ).astype(jnp.float32),
    )
    query_low = rotate_rows(query_grad, cos_table, -sin_table).astype(jnp.bfloat16)
    key_low = rotate_rows(key_grad, cos_table, -sin_table).astype(jnp.bfloat16)
    value_grad_low = value_grad.astype(jnp.bfloat16)
    q_part = jnp.einsum("scd,sce->de", normed_one, query_low, preferred_element_type=jnp.float32)
    k_part = jnp.einsum("scd,sce->de", normed_one, key_low, preferred_element_type=jnp.float32)
    v_part = jnp.einsum(
        "scd,sce->de", normed_one, value_grad_low, preferred_element_type=jnp.float32
    )
    local_normed = jnp.einsum("sce,de->scd", query_low, q_full, preferred_element_type=jnp.float32)
    local_normed = local_normed + jnp.einsum(
        "sce,de->scd", key_low, k_full, preferred_element_type=jnp.float32
    )
    local_normed = local_normed + jnp.einsum(
        "sce,de->scd", value_grad_low, v_full, preferred_element_type=jnp.float32
    )
    grad_normed_one = lax.psum(local_normed.astype(jnp.bfloat16), "tensor").astype(jnp.float32)
    input_part, gain_one_grad = norm_reverse_pass(hidden_in, rms_one, gain_one, grad_normed_one)
    input_grad = (grad_resid + input_part).astype(jnp.bfloat16)
    shares = (
        lax.psum_scatter(gain_one_grad, ("fsdp", "context"), scatter_dimension=0, tiled=True),
        lax.psum_scatter(q_part, ("fsdp", "context"), scatter_dimension=0, tiled=True),
        lax.psum_scatter(k_part, ("fsdp", "context"), scatter_dimension=0, tiled=True),
        lax.psum_scatter(v_part, ("fsdp", "context"), scatter_dimension=0, tiled=True),
        lax.psum_scatter(o_part, ("fsdp", "context"), scatter_dimension=0, tiled=True),
        lax.psum_scatter(gain_two_grad, ("fsdp", "context"), scatter_dimension=0, tiled=True),
    )
    return (
        layer_output,
        input_grad,
        shares[0],
        shares[1],
        shares[2],
        shares[3],
        shares[4],
        shares[5],
        gate_share,
        up_share,
        down_share,
    )


def solution(mesh):
    placed = (
        P("fsdp", "context", None),
        P("fsdp"),
        P(("fsdp", "context")),
        P(("fsdp", "context"), "tensor"),
        P(("fsdp", "context"), "tensor"),
        P(("fsdp", "context"), "tensor"),
        P(("fsdp", "context"), "tensor"),
        P(("fsdp", "context")),
        P(("fsdp", "context"), "tensor"),
        P(("fsdp", "context"), "tensor"),
        P(("fsdp", "context"), "tensor"),
        P("fsdp", "context", None),
    )
    return jax.shard_map(
        on_device,
        mesh=mesh,
        in_specs=placed,
        out_specs=(
            P("fsdp", "context", None),
            P("fsdp", "context", None),
            P(("fsdp", "context")),
            P(("fsdp", "context"), "tensor"),
            P(("fsdp", "context"), "tensor"),
            P(("fsdp", "context"), "tensor"),
            P(("fsdp", "context"), "tensor"),
            P(("fsdp", "context")),
            P(("fsdp", "context"), "tensor"),
            P(("fsdp", "context"), "tensor"),
            P(("fsdp", "context"), "tensor"),
        ),
        check_vma=False,
    )
```

profile of v0, /device:TPU:0, one launch (start us, length us, event | category | flops | bytes accessed | tf_op | source)
XLA Modules:
  0.0 3718.7 jit_solution(15053935400837778976)
XLA Ops:
  14.9 42.2 %all-gather.2 = bf16[16,1,128]{2,1,0:T(2,128)(2,1)S(1)} all-gather(bf16[1,1,128]{2,1,0:T(2,128)(2,1)S(1)} %convert_bitcast_fusion.1), channel_id=1, replica_groups=mesh['fsdp'=4,'context'=4,'tensor'=2] {'fsdp','context'}, dimensions={0}, use_global_device_ids=true | all-gather | bytes 4352 | tf_op jit(solution)/shard_map/all_gather | solution.py:130
  62.0 7.4 all-gather.14.cloned.1.call-done
  71.5 55.5 %all-gather.12.cloned.1.call-done = bf16[2048,256]{1,0:T(8,128)(2,1)} async-done(((bf16[128,256]{1,0:T(8,128)(2,1)}), bf16[2048,256]{1,0:T(8,128)(2,1)}) %all-gather.12.cloned.1.call-update) | async-done | bytes 1048592 | tf_op jit(solution)/shard_map/all_gather | solution.py:133
  128.7 16.9 all-gather
  146.6 16.7 all-gather.1
  163.3 42.9 %all-gather.16.cloned.1.call-done = bf16[2048,1024]{1,0:T(8,128)(2,1)} async-done(((bf16[128,1024]{1,0:T(8,128)(2,1)}), bf16[2048,1024]{1,0:T(8,128)(2,1)}) %all-gather.16.cloned.1.call-update) | async-done | bytes 4194320 | tf_op jit(solution)/shard_map/all_gather | solution.py:131
  206.2 4.5 fusion.71
  213.8 2.6 add_convert_fusion.2
  216.6 7.2 fusion.79
  223.8 8.1 fusion.3
  231.9 7.6 fusion.40
  239.5 44.5 %all-gather.18.cloned.1.call-done = bf16[2048,1024]{1,0:T(8,128)(2,1)} async-done(((bf16[128,1024]{1,0:T(8,128)(2,1)}), bf16[2048,1024]{1,0:T(8,128)(2,1)}) %all-gather.18.cloned.1.call-update) | async-done | bytes 4194320 | tf_op jit(solution)/shard_map/all_gather | solution.py:134
  284.0 4.8 convolution_bitcast_fusion.3
  291.5 2.8 convert_element_type.227
  295.7 38.4 %all-gather.3 = bf16[16,1,128]{2,1,0:T(2,128)(2,1)S(1)} all-gather(bf16[1,1,128]{2,1,0:T(2,128)(2,1)S(1)} %convert_bitcast_fusion), channel_id=1, replica_groups=mesh['fsdp'=4,'context'=4,'tensor'=2] {'fsdp','context'}, dimensions={0}, use_global_device_ids=true | all-gather | bytes 4352 | tf_op jit(solution)/shard_map/all_gather | solution.py:159
  336.3 168.8 %all-gather.22.cloned.1.call-done = bf16[2048,4096]{1,0:T(8,128)(2,1)} async-done(((bf16[128,4096]{1,0:T(8,128)(2,1)}), bf16[2048,4096]{1,0:T(8,128)(2,1)}) %all-gather.22.cloned.1.call-update) | async-done | bytes 16777232 | tf_op jit(solution)/shard_map/all_gather | solution.py:161
  505.2 10.1 fusion.81
  515.2 183.5 %all-gather.20.cloned.1.call-done = bf16[2048,4096]{1,0:T(8,128)(2,1)} async-done(((bf16[128,4096]{1,0:T(8,128)(2,1)}), bf16[2048,4096]{1,0:T(8,128)(2,1)}) %all-gather.20.cloned.1.call-update) | async-done | bytes 16777232 | tf_op jit(solution)/shard_map/all_gather | solution.py:160
  698.7 10.2 fusion.80
  708.9 183.3 %all-gather.24.cloned.1.call-done = bf16[2048,4096]{1,0:T(8,128)(2,1)} async-done(((bf16[128,4096]{1,0:T(8,128)(2,1)}), bf16[2048,4096]{1,0:T(8,128)(2,1)}) %all-gather.24.cloned.1.call-update) | async-done | bytes 16777232 | tf_op jit(solution)/shard_map/all_gather | solution.py:162
  892.2 12.5 multiply_convert_fusion
  904.7 13.1 convolution_bitcast_fusion.1
  917.8 13.5 convolution_bitcast_fusion.2
  931.3 12.2 fusion.82
  943.6 12.5 fusion.15
  956.2 15.4 convolution_bitcast_fusion
  971.6 12.0 fusion.14
  990.8 15.6 fusion
  1006.4 8.2 fusion.2
  1014.7 3.4 fusion.39
  1018.1 2.5 broadcast_multiply_fusion
  1021.9 9.4 fusion.36
  1034.3 2.6 fusion.83
  1036.9 4.1 reduce-scatter.8.cloned.1.call-done
  1045.8 17.5 reduce-scatter.10.cloned.1.call-done
  1063.2 3.4 fusion.16
  1066.7 66.8 %pad_maximum_fusion = f32[2048,3,4096]{2,0,1:T(8,128)} fusion(f32[2048,1,4096]{2,0,1:T(8,128)} %convolution_bitcast_fusion, f32[2048,1,4096]{2,0,1:T(8,128)} %convolution_bitcast_fusion.1, f32[2048,1,4096]{2,0,1:T(8,128)} %convolution_bitcast_fusion.2), kind=kLoop, calls=%fused_computation | loop fusion | flops 50331648 | bytes 201326592 | tf_op jit(solution)/shard_map/concatenate | solution.py:203
  1136.8 2.0 fusion.61
  1138.9 6.4 fusion.45
  1147.9 4.7 fusion.69
  1156.4 78.9 %all-reduce.2 = (f32[2048]{0:T(1024)S(1)}, f32[2048]{0:T(1024)S(1)}) all-reduce(f32[2048]{0:T(1024)S(1)} %get-tuple-element.59, f32[2048]{0:T(1024)S(1)} %get-tuple-element.57), channel_id=6, replica_groups=mesh['fsdp'=4,'context'=4,'tensor'=2] {'fsdp','context'}, use_global_device_ids=true, to_apply=%region_14.15.clone | all-reduce | flops 4096 | bytes 32768
  1236.4 4.2 fusion.19
  1240.6 1936.0 %reduce-scatter.20.cloned.1.call-done = f32[128,3,4096]{2,0,1:T(8,128)} async-done(((f32[2048,3,4096]{2,0,1:T(8,128)}), f32[128,3,4096]{2,0,1:T(8,128)}) %reduce-scatter.20.cloned.1.call-update) | async-done | bytes 6291472 | tf_op jit(solution)/shard_map/reduce_scatter | solution.py:202
  3176.6 5.8 slice_bitcast_fusion
  3182.4 81.5 %reduce-scatter.16.cloned.1.call-done = f32[128,256]{1,0:T(8,128)} async-done(((f32[2048,256]{1,0:T(8,128)}), f32[128,256]{1,0:T(8,128)}) %reduce-scatter.16.cloned.1.call-update) | async-done | bytes 131088 | tf_op jit(solution)/shard_map/reduce_scatter | solution.py:263
  3263.8 83.6 %reduce-scatter.14.cloned.1.call-done = f32[128,256]{1,0:T(8,128)} async-done(((f32[2048,256]{1,0:T(8,128)}), f32[128,256]{1,0:T(8,128)}) %reduce-scatter.14.cloned.1.call-update) | async-done | bytes 131088 | tf_op jit(solution)/shard_map/reduce_scatter | solution.py:262
  3347.5 181.9 %reduce-scatter.18.cloned.1.call-done = f32[128,1024]{1,0:T(8,128)} async-done(((f32[2048,1024]{1,0:T(8,128)}), f32[128,1024]{1,0:T(8,128)}) %reduce-scatter.18.cloned.1.call-update) | async-done | bytes 524304 | tf_op jit(solution)/shard_map/reduce_scatter | solution.py:264
  3529.3 182.6 %reduce-scatter.12.cloned.1.call-done = f32[128,1024]{1,0:T(8,128)} async-done(((f32[2048,1024]{1,0:T(8,128)}), f32[128,1024]{1,0:T(8,128)}) %reduce-scatter.12.cloned.1.call-update) | async-done | bytes 524304 | tf_op jit(solution)/shard_map/reduce_scatter | solution.py:261
  (172 shorter events, 52.4 us)
Async XLA Ops:
  7.2 7.7 copy-start.31
  7.2 62.3 %all-gather.14.cloned.1.call-start = ((), (), s32[]{:S(2)}) async-start(), calls=%async_computation.8 | async-start | bytes 1114112 | tf_op jit(solution)/shard_map/all_gather | solution.py:132
  8.8 118.2 %all-gather.12.cloned.1.call-start = ((), (), s32[]{:S(2)}) async-start(), calls=%async_computation.7 | async-start | bytes 1114112 | tf_op jit(solution)/shard_map/all_gather | solution.py:133
  10.4 195.8 %all-gather.16.cloned.1.call-start = ((), (), s32[]{:S(2)}) async-start(), calls=%async_computation.9 | async-start | bytes 4456448 | tf_op jit(solution)/shard_map/all_gather | solution.py:131
  12.3 271.7 %all-gather.18.cloned.1.call-start = ((), (), s32[]{:S(2)}) async-start(), calls=%async_computation.10 | async-start | bytes 4456448 | tf_op jit(solution)/shard_map/all_gather | solution.py:134
  14.1 320.0 %all-reduce.8.cloned.1.call-start = ((), (), s32[]{:S(2)}) async-start(), calls=%async_computation.11 | async-start | bytes 4194304 | tf_op jit(solution)/shard_map/psum | solution.py:153
  57.1 149.1 %copy-start.21 = (f32[16,1,128]{2,1,0:T(1,128)}, f32[16,1,128]{2,1,0:T(1,128)S(1)}, u32[]{:S(2)}) copy-start(f32[16,1,128]{2,1,0:T(1,128)S(1)} %convert_element_type.260) | copy-start | bytes 24580
  58.1 13.3 copy-start.17
  59.5 1.4 copy-start
  61.8 144.4 %copy-start.26 = (f32[256]{0:T(256)}, f32[256]{0:T(256)S(1)}, u32[]{:S(2)}) copy-start(f32[256]{0:T(256)S(1)} %get-tuple-element.97) | copy-start | bytes 3076
  163.3 53.2 %copy-start.7 = (bf16[1024,256]{0,1:T(8,128)(2,1)}, bf16[1024,256]{0,1:T(8,128)(2,1)S(1)}, u32[]{:S(2)}) copy-start(bf16[1024,256]{0,1:T(8,128)(2,1)S(1)} %all-gather.1) | copy-start | bytes 1572868
  216.5 7.2 copy-start.5
  223.8 8.1 copy-start.11
  239.5 44.5 %copy-start.23 = (bf16[4,64,4,256]{3,1,2,0:T(8,128)(2,1)}, bf16[4,64,4,256]{3,1,2,0:T(8,128)(2,1)S(1)}, u32[]{:S(2)}) copy-start(bf16[4,64,4,256]{3,1,2,0:T(8,128)(2,1)S(1)} %fusion.40) | copy-start | bytes 1572868
  288.8 1.6 copy-start.14
  288.8 216.4 %all-gather.22.cloned.1.call-start = ((), (), s32[]{:S(2)}) async-start(), calls=%async_computation.13 | async-start | bytes 17825792 | tf_op jit(solution)/shard_map/all_gather | solution.py:161
  291.5 3.0 copy-start.15
  291.5 407.2 %all-gather.20.cloned.1.call-start = ((), (), s32[]{:S(2)}) async-start(), calls=%async_computation.12 | async-start | bytes 17825792 | tf_op jit(solution)/shard_map/all_gather | solution.py:160
  294.4 1.2 copy-start.32
  294.4 597.8 %all-gather.24.cloned.1.call-start = ((), (), s32[]{:S(2)}) async-start(), calls=%async_computation.14 | async-start | bytes 17825792 | tf_op jit(solution)/shard_map/all_gather | solution.py:162
  295.6 688.0 %all-reduce.10.cloned.1.call-start = ((), (), s32[]{:S(2)}) async-start(), calls=%async_computation.15 | async-start | bytes 2097152 | tf_op jit(solution)/shard_map/psum | solution.py:189
  904.7 13.1 copy-start.12
  904.7 13.1 copy-start.13
  943.6 12.6 copy-start.9
  956.1 84.8 %reduce-scatter.8.cloned.1.call-start = ((), (), s32[]{:S(2)}) async-start(), calls=%async_computation.16 | async-start | bytes 655360 | tf_op jit(solution)/shard_map/reduce_scatter | solution.py:234
  983.6 2.0 copy-start.10
  985.6 2.9 copy-start.30
  986.3 1.3 copy-start.2
  990.8 15.6 slice-start
  990.8 15.6 slice-start.1
  990.8 15.6 slice-start.2
  990.8 15.6 slice-start.3
  1006.4 8.2 copy-start.6
  1014.7 3.4 copy-start.8
  1020.6 42.6 %reduce-scatter.10.cloned.1.call-start = ((), (), s32[]{:S(2)}) async-start(), calls=%async_computation.17 | async-start | bytes 655360 | tf_op jit(solution)/shard_map/reduce_scatter | solution.py:237
  1031.3 2.5 copy-start.18
  1031.3 2.5 copy-start.19
  1031.3 123.2 %all-reduce.12.cloned.1.call-start = ((), (), s32[]{:S(2)}) async-start(), calls=%async_computation.23 | async-start | bytes 4194304 | tf_op jit(solution)/shard_map/psum | solution.py:170
  1031.3 2.9 copy-start.29
  1034.3 9.7 copy-start.20
  1041.0 3.0 copy-start.16
  1066.7 2109.9 %reduce-scatter.20.cloned.1.call-start = ((), (), s32[]{:S(2)}) async-start(), calls=%async_computation.22 | async-start | bytes 106954752 | tf_op jit(solution)/shard_map/reduce_scatter | solution.py:202
  1133.5 1.2 copy-start.1
  1133.6 2130.2 %reduce-scatter.16.cloned.1.call-start = ((), (), s32[]{:S(2)}) async-start(), calls=%async_computation.20 | async-start | bytes 2228224 | tf_op jit(solution)/shard_map/reduce_scatter | solution.py:263
  1136.8 2210.7 %reduce-scatter.14.cloned.1.call-start = ((), (), s32[]{:S(2)}) async-start(), calls=%async_computation.19 | async-start | bytes 2228224 | tf_op jit(solution)/shard_map/reduce_scatter | solution.py:262
  1138.9 2390.5 %reduce-scatter.18.cloned.1.call-start = ((), (), s32[]{:S(2)}) async-start(), calls=%async_computation.21 | async-start | bytes 8912896 | tf_op jit(solution)/shard_map/reduce_scatter | solution.py:264
  1145.4 2566.5 %reduce-scatter.12.cloned.1.call-start = ((), (), s32[]{:S(2)}) async-start(), calls=%async_computation.18 | async-start | bytes 8912896 | tf_op jit(solution)/shard_map/reduce_scatter | solution.py:261
  1152.6 83.8 %copy-start.28 = (f32[256]{0:T(256)S(1)}, f32[256]{0:T(256)}, u32[]{:S(2)}) copy-start(f32[256]{0:T(256)} %get-tuple-element.96) | copy-start | bytes 3076
  (7 other events, 7.3 us)
Sparse Core Ops, SparseCore 0:
  11.3 58.0 all-gather.13
  72.8 54.1 all-gather.11
  130.3 75.8 all-gather.15
  209.4 74.5 all-gather.17
  288.9 19.7 all-reduce.7
  312.3 192.7 all-gather.21
  508.9 189.7 all-gather.19
  702.4 189.7 all-gather.23
  956.3 17.7 all-reduce.9
  1020.8 20.1 reduce-scatter.7
  1043.2 19.9 reduce-scatter.9
  1066.8 19.6 all-reduce.11
  1133.7 2042.8 reduce-scatter.19
  3179.3 84.4 reduce-scatter.15
  3266.5 80.8 reduce-scatter.13
  3350.2 179.1 reduce-scatter.17
  3532.1 179.8 reduce-scatter.11
where the time goes:
time: 3720 us
  waiting for transfers between devices  3170 us (85%)
  matrix products  194 us (5%)
  blocking collectives  193 us (5%)
  other arithmetic  117 us (3%)
    reduce_scatter x1, waiting for transfers between devices, on_device(): lax.psum_scatter(jnp.concatenate([pair_part, down_part[:, None, :]], axis...  1940 us
    all_gather x1, waiting for transfers between devices, on_device(): lax.all_gather(gate_weight.astype(jnp.bfloat16), ('fsdp', 'context'), axi...  183 us
    all_gather x1, waiting for transfers between devices, on_device(): lax.all_gather(down_weight.astype(jnp.bfloat16), ('fsdp', 'context'), axi...  183 us
    reduce_scatter x1, waiting for transfers between devices, on_device(): lax.psum_scatter(q_part, ('fsdp', 'context'), scatter_dimension=0, tiled=...  183 us
    reduce_scatter x1, waiting for transfers between devices, on_device(): lax.psum_scatter(o_part, ('fsdp', 'context'), scatter_dimension=0, tiled=...  182 us
    all_gather x1, waiting for transfers between devices, on_device(): lax.all_gather(up_weight.astype(jnp.bfloat16), ('fsdp', 'context'), axis=...  169 us
    reduce_scatter x1, waiting for transfers between devices, on_device(): lax.psum_scatter(k_part, ('fsdp', 'context'), scatter_dimension=0, tiled=...  83.6 us
    reduce_scatter x1, waiting for transfers between devices, on_device(): lax.psum_scatter(v_part, ('fsdp', 'context'), scatter_dimension=0, tiled=...  81.5 us
  transfers between devices with their start and end apart: 17, of which 14 were waited for; matrix products, arithmetic and copies ran while one was open for 6% of the time, Pallas kernels for 0%

commit v1 on v0

--- a/solution.py
+++ b/solution.py
@@ -9,6 +9,28 @@
 KV_HEADS = 8
 HEAD_DIM = 64
 EPS = 1e-05
+
+
+def in_order(tiles, dim):
+    shape = list(tiles.shape[1:])
+    shape[dim] *= tiles.shape[0]
+    return jnp.moveaxis(tiles, 0, dim).reshape(shape)
+
+
+def gather_around(x, axis, dim):
+    size = lax.axis_size(axis)
+    pairs = [(i, (i + 1) % size) for i in range(size)]
+    back = [(b, a) for a, b in pairs]
+    lower, upper = ([], [])
+    for step in range(size - 1):
+        if step % 2 == 0:
+            lower.append(lax.ppermute(lower[-1] if lower else x, axis, pairs))
+        else:
+            upper.append(lax.ppermute(upper[-1] if upper else x, axis, back))
+    pieces = jnp.stack([*lower[::-1], x, *upper])
+    shift = lax.axis_index(axis) - len(lower)
+    pieces = pieces[(jnp.arange(size) - shift) % size]
+    return in_order(pieces, dim)
 
 
 def rope_tables(length, head_dim):
@@ -158,7 +180,7 @@
     gain_two, gate_full, up_full, down_full = (
         lax.all_gather(mlp_gain.astype(jnp.bfloat16), ("fsdp", "context"), axis=0, tiled=True),
         lax.all_gather(gate_weight.astype(jnp.bfloat16), ("fsdp", "context"), axis=0, tiled=True),
-        lax.all_gather(up_weight.astype(jnp.bfloat16), ("fsdp", "context"), axis=0, tiled=True),
+        gather_around(up_weight.astype(jnp.bfloat16), ("fsdp", "context"), 0),
         lax.all_gather(down_weight.astype(jnp.bfloat16), ("fsdp", "context"), axis=0, tiled=True),
     )
     normed_two, rms_two = norm_forward(resid, gain_two)

time: 3720 us -> 3930 us (1.056)
  starting transfers between devices: 0.96 us -> 105 us
  blocking collectives: 193 us -> 262 us
    ppermute x0 -> x15, waiting for transfers between devices: none -> 411 us  [the longest x8 252 us: gather_around(): lower.append(lax.ppermute(lower[-1] if lower else x, axis, pairs))]
    all_gather x1, waiting for transfers between devices: 183 us -> 0.01 us  [on_device(): lax.all_gather(gate_weight.astype(jnp.bfloat16), ('fsdp', 'context'), axi...]
    all_gather x1, waiting for transfers between devices: 183 us -> 0.02 us  [on_device(): lax.all_gather(down_weight.astype(jnp.bfloat16), ('fsdp', 'context'), axi...]
    ppermute x0 -> x15, starting transfers between devices: none -> 104 us  [the longest x8 84.9 us: gather_around(): lower.append(lax.ppermute(lower[-1] if lower else x, axis, pairs))]
    all_gather x1, blocking collectives: 38.4 us -> 107 us  [on_device(): lax.all_gather(mlp_gain.astype(jnp.bfloat16), ('fsdp', 'context'), axis=0...]
    all_gather x1, waiting for transfers between devices: 169 us -> 121 us  [on_device(): lax.all_gather(up_weight.astype(jnp.bfloat16), ('fsdp', 'context'), axis=...]
  transfers between devices with their start and end apart: 17 -> 32, of which waited for: 14 -> 25; matrix products, arithmetic and copies ran while one was open for 6% -> 8% of each run, Pallas kernels for 0% -> 0%
where the time goes in v1:
time: 3930 us
  waiting for transfers between devices  3170 us (81%)
  blocking collectives  262 us (7%)
  matrix products  196 us (5%)
  other arithmetic  122 us (3%)
  starting transfers between devices  105 us (3%)
  local copies, waits for them, and re-layouts  60.5 us (2%)
    reduce_scatter x1, waiting for transfers between devices, on_device(): lax.psum_scatter(jnp.concatenate([pair_part, down_part[:, None, :]], axis...  1940 us
    ppermute x8, waiting for transfers between devices, gather_around(): lower.append(lax.ppermute(lower[-1] if lower else x, axis, pairs))  252 us
    reduce_scatter x1, waiting for transfers between devices, on_device(): lax.psum_scatter(q_part, ('fsdp', 'context'), scatter_dimension=0, tiled=...  183 us
    reduce_scatter x1, waiting for transfers between devices, on_device(): lax.psum_scatter(o_part, ('fsdp', 'context'), scatter_dimension=0, tiled=...  182 us
    ppermute x7, waiting for transfers between devices, gather_around(): upper.append(lax.ppermute(upper[-1] if upper else x, axis, back))  159 us
    all_gather x1, waiting for transfers between devices, on_device(): lax.all_gather(up_weight.astype(jnp.bfloat16), ('fsdp', 'context'), axis=...  121 us
    all_gather x1, blocking collectives, on_device(): lax.all_gather(mlp_gain.astype(jnp.bfloat16), ('fsdp', 'context'), axis=0...  107 us
    ppermute x8, starting transfers between devices, gather_around(): lower.append(lax.ppermute(lower[-1] if lower else x, axis, pairs))  84.9 us
  transfers between devices with their start and end apart: 32, of which 25 were waited for; matrix products, arithmetic and copies ran while one was open for 8% of the time, Pallas kernels for 0%

profile of v1, /device:TPU:0, one launch (start us, length us, event | category | flops | bytes accessed | tf_op | source)
XLA Modules:
  0.0 3927.1 jit_solution(6090260077784476551)
XLA Ops:
  15.6 42.2 %all-gather.2 = bf16[16,1,128]{2,1,0:T(2,128)(2,1)S(1)} all-gather(bf16[1,1,128]{2,1,0:T(2,128)(2,1)S(1)} %convert_bitcast_fusion.1), channel_id=1, replica_groups=mesh['fsdp'=4,'context'=4,'tensor'=2] {'fsdp','context'}, dimensions={0}, use_global_device_ids=true | all-gather | bytes 4352 | tf_op jit(solution)/shard_map/all_gather | solution.py:152
  71.4 55.5 %all-gather.12.cloned.1.call-done = bf16[2048,256]{1,0:T(8,128)(2,1)} async-done(((bf16[128,256]{1,0:T(8,128)(2,1)}), bf16[2048,256]{1,0:T(8,128)(2,1)}) %all-gather.12.cloned.1.call-update) | async-done | bytes 1048592 | tf_op jit(solution)/shard_map/all_gather | solution.py:155
  128.7 16.9 all-gather
  146.6 17.0 all-gather.1
  163.5 42.7 %all-gather.16.cloned.1.call-done = bf16[2048,1024]{1,0:T(8,128)(2,1)} async-done(((bf16[128,1024]{1,0:T(8,128)(2,1)}), bf16[2048,1024]{1,0:T(8,128)(2,1)}) %all-gather.16.cloned.1.call-update) | async-done | bytes 4194320 | tf_op jit(solution)/shard_map/all_gather | solution.py:153
  216.6 7.3 fusion.81
  223.9 8.1 fusion.3
  231.9 7.6 fusion.40
  239.6 44.4 %all-gather.18.cloned.1.call-done = bf16[2048,1024]{1,0:T(8,128)(2,1)} async-done(((bf16[128,1024]{1,0:T(8,128)(2,1)}), bf16[2048,1024]{1,0:T(8,128)(2,1)}) %all-gather.18.cloned.1.call-update) | async-done | bytes 4194320 | tf_op jit(solution)/shard_map/all_gather | solution.py:156
  297.3 26.1 collective-permute-done
  328.9 45.8 %collective-permute-done.1 = bf16[128,4096]{1,0:T(8,128)(2,1)S(1)} collective-permute-done((bf16[128,4096]{1,0:T(8,128)(2,1)}, bf16[128,4096]{1,0:T(8,128)(2,1)S(1)}, u32[]{:S(2)}, u32[]{:S(2)}) %collective-permute-start.1) | collective-permute-done | bytes 1048608 | tf_op jit(solution)/shard_map/ppermute | solution.py:27
  374.7 33.9 collective-permute-done.8
  409.5 38.0 collective-permute-done.2
  447.5 26.4 collective-permute-start.3
  473.9 7.6 collective-permute-done.9
  487.2 42.2 %collective-permute-done.3 = bf16[128,4096]{1,0:T(8,128)(2,1)S(1)} collective-permute-done((bf16[128,4096]{1,0:T(8,128)(2,1)S(1)}, bf16[128,4096]{1,0:T(8,128)(2,1)S(1)}, u32[]{:S(2)}, u32[]{:S(2)}) %collective-permute-start.3) | collective-permute-done | bytes 1048608 | tf_op jit(solution)/shard_map/ppermute | solution.py:27
  529.4 27.2 collective-permute-start.4
  556.6 18.7 collective-permute-done.10
  576.2 43.1 %collective-permute-done.4 = bf16[128,4096]{1,0:T(8,128)(2,1)S(1)} collective-permute-done((bf16[128,4096]{1,0:T(8,128)(2,1)S(1)}, bf16[128,4096]{1,0:T(8,128)(2,1)S(1)}, u32[]{:S(2)}, u32[]{:S(2)}) %collective-permute-start.4) | collective-permute-done | bytes 1048608 | tf_op jit(solution)/shard_map/ppermute | solution.py:27
  619.3 29.8 collective-permute-start.5
  649.0 16.5 collective-permute-done.11
  666.6 25.8 collective-permute-done.5
  692.4 40.0 %collective-permute-done.12 = bf16[128,4096]{1,0:T(8,128)(2,1)} collective-permute-done((bf16[128,4096]{1,0:T(8,128)(2,1)S(1)}, bf16[128,4096]{1,0:T(8,128)(2,1)}, u32[]{:S(2)}, u32[]{:S(2)}) %collective-permute-start.12) | collective-permute-done | bytes 1048608 | tf_op jit(solution)/shard_map/ppermute | solution.py:29
  734.6 30.9 collective-permute-done.6
  765.5 107.1 %all-gather.3 = bf16[16,1,128]{2,1,0:T(2,128)(2,1)S(1)} all-gather(bf16[1,1,128]{2,1,0:T(2,128)(2,1)S(1)} %convert_bitcast_fusion), channel_id=1, replica_groups=mesh['fsdp'=4,'context'=4,'tensor'=2] {'fsdp','context'}, dimensions={0}, use_global_device_ids=true | all-gather | bytes 4352 | tf_op jit(solution)/shard_map/all_gather | solution.py:181
  900.9 42.4 %collective-permute-done.14 = bf16[128,4096]{1,0:T(8,128)(2,1)S(1)} collective-permute-done((bf16[128,4096]{1,0:T(8,128)(2,1)}, bf16[128,4096]{1,0:T(8,128)(2,1)S(1)}, u32[]{:S(2)}, u32[]{:S(2)}) %collective-permute-start.14) | collective-permute-done | bytes 1048608 | tf_op jit(solution)/shard_map/ppermute | solution.py:29
  944.3 13.7 gather_fusion
  960.3 12.6 fusion.49
  972.9 8.3 fusion.82
  981.2 10.7 multiply_convert_fusion
  991.9 13.9 convolution_bitcast_fusion.1
  1005.8 13.4 convolution_bitcast_fusion.2
  1019.3 12.3 fusion.83
  1031.5 120.7 %all-gather.24.cloned.1.call-done = bf16[2048,4096]{1,0:T(8,128)(2,1)} async-done(((bf16[128,4096]{1,0:T(8,128)(2,1)}), bf16[2048,4096]{1,0:T(8,128)(2,1)}) %all-gather.24.cloned.1.call-update) | async-done | bytes 16777232 | tf_op jit(solution)/shard_map/all_gather | solution.py:202
  1152.3 12.4 fusion.15
  1164.8 15.4 convolution_bitcast_fusion
  1180.2 12.0 fusion.14
  1199.8 15.6 fusion
  1215.4 8.4 fusion.2
  1230.9 9.6 fusion.36
  1256.3 16.0 reduce-scatter.10.cloned.1.call-done
  1275.8 66.8 %pad_maximum_fusion = f32[2048,3,4096]{2,0,1:T(8,128)} fusion(f32[2048,1,4096]{2,0,1:T(8,128)} %convolution_bitcast_fusion, f32[2048,1,4096]{2,0,1:T(8,128)} %convolution_bitcast_fusion.1, f32[2048,1,4096]{2,0,1:T(8,128)} %convolution_bitcast_fusion.2), kind=kLoop, calls=%fused_computation.1 | loop fusion | flops 50331648 | bytes 201326592 | tf_op jit(solution)/shard_map/concatenate | solution.py:225
  1365.3 79.0 %all-reduce.2 = (f32[2048]{0:T(1024)S(1)}, f32[2048]{0:T(1024)S(1)}) all-reduce(f32[2048]{0:T(1024)S(1)} %get-tuple-element.59, f32[2048]{0:T(1024)S(1)} %get-tuple-element.57), channel_id=6, replica_groups=mesh['fsdp'=4,'context'=4,'tensor'=2] {'fsdp','context'}, use_global_device_ids=true, to_apply=%region_14.15.clone | all-reduce | flops 4096 | bytes 32768
  1449.6 1935.5 %reduce-scatter.20.cloned.1.call-done = f32[128,3,4096]{2,0,1:T(8,128)} async-done(((f32[2048,3,4096]{2,0,1:T(8,128)}), f32[128,3,4096]{2,0,1:T(8,128)}) %reduce-scatter.20.cloned.1.call-update) | async-done | bytes 6291472 | tf_op jit(solution)/shard_map/reduce_scatter | solution.py:224
  3390.9 81.7 %reduce-scatter.16.cloned.1.call-done = f32[128,256]{1,0:T(8,128)} async-done(((f32[2048,256]{1,0:T(8,128)}), f32[128,256]{1,0:T(8,128)}) %reduce-scatter.16.cloned.1.call-update) | async-done | bytes 131088 | tf_op jit(solution)/shard_map/reduce_scatter | solution.py:285
  3472.6 83.7 %reduce-scatter.14.cloned.1.call-done = f32[128,256]{1,0:T(8,128)} async-done(((f32[2048,256]{1,0:T(8,128)}), f32[128,256]{1,0:T(8,128)}) %reduce-scatter.14.cloned.1.call-update) | async-done | bytes 131088 | tf_op jit(solution)/shard_map/reduce_scatter | solution.py:284
  3556.2 181.6 %reduce-scatter.18.cloned.1.call-done = f32[128,1024]{1,0:T(8,128)} async-done(((f32[2048,1024]{1,0:T(8,128)}), f32[128,1024]{1,0:T(8,128)}) %reduce-scatter.18.cloned.1.call-update) | async-done | bytes 524304 | tf_op jit(solution)/shard_map/reduce_scatter | solution.py:286
  3737.8 182.6 %reduce-scatter.12.cloned.1.call-done = f32[128,1024]{1,0:T(8,128)} async-done(((f32[2048,1024]{1,0:T(8,128)}), f32[128,1024]{1,0:T(8,128)}) %reduce-scatter.12.cloned.1.call-update) | async-done | bytes 524304 | tf_op jit(solution)/shard_map/reduce_scatter | solution.py:283
  (249 shorter events, 162.3 us)
Async XLA Ops:
  7.2 62.3 %all-gather.14.cloned.1.call-start = ((), (), s32[]{:S(2)}) async-start(), calls=%async_computation.8 | async-start | bytes 1114112 | tf_op jit(solution)/shard_map/all_gather | solution.py:154
  8.8 118.2 %all-gather.12.cloned.1.call-start = ((), (), s32[]{:S(2)}) async-start(), calls=%async_computation.7 | async-start | bytes 1114112 | tf_op jit(solution)/shard_map/all_gather | solution.py:155
  10.4 195.9 %all-gather.16.cloned.1.call-start = ((), (), s32[]{:S(2)}) async-start(), calls=%async_computation.9 | async-start | bytes 4456448 | tf_op jit(solution)/shard_map/all_gather | solution.py:153
  12.2 49.4 %copy-start = (bf16[1,256,2048]{2,1,0:T(8,128)(2,1)S(1)}, bf16[1,256,2048]{2,1,0:T(8,128)(2,1)}, u32[]{:S(2)}) copy-start(bf16[1,256,2048]{2,1,0:T(8,128)(2,1)} %param.12) | copy-start | bytes 3145732
  12.3 271.7 %all-gather.18.cloned.1.call-start = ((), (), s32[]{:S(2)}) async-start(), calls=%async_computation.10 | async-start | bytes 4456448 | tf_op jit(solution)/shard_map/all_gather | solution.py:156
  14.2 943.8 %all-reduce.8.cloned.1.call-start = ((), (), s32[]{:S(2)}) async-start(), calls=%async_computation.11 | async-start | bytes 4194304 | tf_op jit(solution)/shard_map/psum | solution.py:175
  57.8 148.5 %copy-start.35 = (f32[16,1,128]{2,1,0:T(1,128)}, f32[16,1,128]{2,1,0:T(1,128)S(1)}, u32[]{:S(2)}) copy-start(f32[16,1,128]{2,1,0:T(1,128)S(1)} %convert_element_type.260) | copy-start | bytes 24580
  62.5 143.8 %copy-start.40 = (f32[256]{0:T(256)}, f32[256]{0:T(256)S(1)}, u32[]{:S(2)}) copy-start(f32[256]{0:T(256)S(1)} %get-tuple-element.97) | copy-start | bytes 3076
  163.5 53.1 %copy-start.7 = (bf16[1024,256]{0,1:T(8,128)(2,1)}, bf16[1024,256]{0,1:T(8,128)(2,1)S(1)}, u32[]{:S(2)}) copy-start(bf16[1024,256]{0,1:T(8,128)(2,1)S(1)} %all-gather.1) | copy-start | bytes 1572868
  239.6 49.2 %copy-start.37 = (bf16[4,64,4,256]{3,1,2,0:T(8,128)(2,1)}, bf16[4,64,4,256]{3,1,2,0:T(8,128)(2,1)S(1)}, u32[]{:S(2)}) copy-start(bf16[4,64,4,256]{3,1,2,0:T(8,128)(2,1)S(1)} %fusion.40) | copy-start | bytes 1572868
  288.8 671.4 %all-gather.22.cloned.1.call-start = ((), (), s32[]{:S(2)}) async-start(), calls=%async_computation.13 | async-start | bytes 17825792 | tf_op jit(solution)/shard_map/all_gather | solution.py:184
  291.7 473.7 %copy-start.45 = (f32[128]{0:T(128)S(1)}, f32[128]{0:T(128)}, u32[]{:S(2)}) copy-start(f32[128]{0:T(128)} %param.19) | copy-start | bytes 1540
  291.8 681.1 %all-gather.20.cloned.1.call-start = ((), (), s32[]{:S(2)}) async-start(), calls=%async_computation.12 | async-start | bytes 17825792 | tf_op jit(solution)/shard_map/all_gather | solution.py:182
  294.5 857.7 %all-gather.24.cloned.1.call-start = ((), (), s32[]{:S(2)}) async-start(), calls=%async_computation.14 | async-start | bytes 17825792 | tf_op jit(solution)/shard_map/all_gather | solution.py:202
  295.7 27.6 collective-permute-start
  297.2 895.1 %all-reduce.10.cloned.1.call-start = ((), (), s32[]{:S(2)}) async-start(), calls=%async_computation.15 | async-start | bytes 2097152 | tf_op jit(solution)/shard_map/psum | solution.py:211
  323.3 51.4 %collective-permute-start.1 = (bf16[128,4096]{1,0:T(8,128)(2,1)}, bf16[128,4096]{1,0:T(8,128)(2,1)S(1)}, u32[]{:S(2)}, u32[]{:S(2)}) collective-permute-start(bf16[128,4096]{1,0:T(8,128)(2,1)} %collective-permute-done), channel_id=1, source_target_pairs={{0,2},{2,4},{4,6},{6,8},{8,10},{10,12},{12,14},{14,16},{16,18},{18... | collective-permute-start | bytes 3145736 | tf_op jit(solution)/shard_map/ppermute | solution.py:27
  323.3 85.2 %collective-permute-start.8 = (bf16[128,4096]{1,0:T(8,128)(2,1)}, bf16[128,4096]{1,0:T(8,128)(2,1)S(1)}, u32[]{:S(2)}, u32[]{:S(2)}) collective-permute-start(bf16[128,4096]{1,0:T(8,128)(2,1)} %convert_element_type.228), channel_id=1, source_target_pairs={{2,0},{4,2},{6,4},{8,6},{10,8},{12,10},{14,12},{16,14},{18,16},{20... | collective-permute-start | bytes 3145736 | tf_op jit(solution)/shard_map/ppermute | solution.py:29
  374.7 106.8 %copy-start.18 = (bf16[128,4096]{1,0:T(8,128)(2,1)}, bf16[128,4096]{1,0:T(8,128)(2,1)S(1)}, u32[]{:S(2)}) copy-start(bf16[128,4096]{1,0:T(8,128)(2,1)S(1)} %collective-permute-done.1) | copy-start | bytes 3145732
  374.7 72.8 %collective-permute-start.2 = (bf16[128,4096]{1,0:T(8,128)(2,1)S(1)}, bf16[128,4096]{1,0:T(8,128)(2,1)S(1)}, u32[]{:S(2)}, u32[]{:S(2)}) collective-permute-start(bf16[128,4096]{1,0:T(8,128)(2,1)S(1)} %collective-permute-done.1), channel_id=1, source_target_pairs={{0,2},{2,4},{4,6},{6,8},{8,10},{10,12},{12,14},{14,16},{16,18},{18... | collective-permute-start | bytes 3145736 | tf_op jit(solution)/shard_map/ppermute | solution.py:27
  409.5 72.0 %collective-permute-start.9 = (bf16[128,4096]{1,0:T(8,128)(2,1)S(1)}, bf16[128,4096]{1,0:T(8,128)(2,1)S(1)}, u32[]{:S(2)}, u32[]{:S(2)}) collective-permute-start(bf16[128,4096]{1,0:T(8,128)(2,1)S(1)} %collective-permute-done.8), channel_id=1, source_target_pairs={{2,0},{4,2},{6,4},{8,6},{10,8},{12,10},{14,12},{16,14},{18,16},{20... | collective-permute-start | bytes 3145736 | tf_op jit(solution)/shard_map/ppermute | solution.py:29
  447.5 127.7 %copy-start.22 = (bf16[128,4096]{1,0:T(8,128)(2,1)}, bf16[128,4096]{1,0:T(8,128)(2,1)S(1)}, u32[]{:S(2)}) copy-start(bf16[128,4096]{1,0:T(8,128)(2,1)S(1)} %collective-permute-done.2) | copy-start | bytes 3145732
  447.5 81.9 %collective-permute-start.3 = (bf16[128,4096]{1,0:T(8,128)(2,1)S(1)}, bf16[128,4096]{1,0:T(8,128)(2,1)S(1)}, u32[]{:S(2)}, u32[]{:S(2)}) collective-permute-start(bf16[128,4096]{1,0:T(8,128)(2,1)S(1)} %collective-permute-done.2), channel_id=1, source_target_pairs={{0,2},{2,4},{4,6},{6,8},{8,10},{10,12},{12,14},{14,16},{16,18},{18... | collective-permute-start | bytes 3145736 | tf_op jit(solution)/shard_map/ppermute | solution.py:27
  481.5 93.7 %collective-permute-start.10 = (bf16[128,4096]{1,0:T(8,128)(2,1)S(1)}, bf16[128,4096]{1,0:T(8,128)(2,1)S(1)}, u32[]{:S(2)}, u32[]{:S(2)}) collective-permute-start(bf16[128,4096]{1,0:T(8,128)(2,1)S(1)} %collective-permute-done.9), channel_id=1, source_target_pairs={{2,0},{4,2},{6,4},{8,6},{10,8},{12,10},{14,12},{16,14},{18,16},{20... | collective-permute-start | bytes 3145736 | tf_op jit(solution)/shard_map/ppermute | solution.py:29
  529.4 203.0 %copy-start.28 = (bf16[128,4096]{1,0:T(8,128)(2,1)}, bf16[128,4096]{1,0:T(8,128)(2,1)S(1)}, u32[]{:S(2)}) copy-start(bf16[128,4096]{1,0:T(8,128)(2,1)S(1)} %collective-permute-done.3) | copy-start | bytes 3145732
  529.4 89.9 %collective-permute-start.4 = (bf16[128,4096]{1,0:T(8,128)(2,1)S(1)}, bf16[128,4096]{1,0:T(8,128)(2,1)S(1)}, u32[]{:S(2)}, u32[]{:S(2)}) collective-permute-start(bf16[128,4096]{1,0:T(8,128)(2,1)S(1)} %collective-permute-done.3), channel_id=1, source_target_pairs={{0,2},{2,4},{4,6},{6,8},{8,10},{10,12},{12,14},{14,16},{16,18},{18... | collective-permute-start | bytes 3145736 | tf_op jit(solution)/shard_map/ppermute | solution.py:27
  575.2 90.3 %collective-permute-start.11 = (bf16[128,4096]{1,0:T(8,128)(2,1)S(1)}, bf16[128,4096]{1,0:T(8,128)(2,1)S(1)}, u32[]{:S(2)}, u32[]{:S(2)}) collective-permute-start(bf16[128,4096]{1,0:T(8,128)(2,1)S(1)} %collective-permute-done.10), channel_id=1, source_target_pairs={{2,0},{4,2},{6,4},{8,6},{10,8},{12,10},{14,12},{16,14},{18,16},{20... | collective-permute-start | bytes 3145736 | tf_op jit(solution)/shard_map/ppermute | solution.py:29
  619.3 115.3 %copy-start.30 = (bf16[128,4096]{1,0:T(8,128)(2,1)}, bf16[128,4096]{1,0:T(8,128)(2,1)S(1)}, u32[]{:S(2)}) copy-start(bf16[128,4096]{1,0:T(8,128)(2,1)S(1)} %collective-permute-done.4) | copy-start | bytes 3145732
  619.3 73.1 %collective-permute-start.5 = (bf16[128,4096]{1,0:T(8,128)(2,1)S(1)}, bf16[128,4096]{1,0:T(8,128)(2,1)S(1)}, u32[]{:S(2)}, u32[]{:S(2)}) collective-permute-start(bf16[128,4096]{1,0:T(8,128)(2,1)S(1)} %collective-permute-done.4), channel_id=1, source_target_pairs={{0,2},{2,4},{4,6},{6,8},{8,10},{10,12},{12,14},{14,16},{16,18},{18... | collective-permute-start | bytes 3145736 | tf_op jit(solution)/shard_map/ppermute | solution.py:27
  666.5 65.8 %collective-permute-start.12 = (bf16[128,4096]{1,0:T(8,128)(2,1)S(1)}, bf16[128,4096]{1,0:T(8,128)(2,1)}, u32[]{:S(2)}, u32[]{:S(2)}) collective-permute-start(bf16[128,4096]{1,0:T(8,128)(2,1)S(1)} %collective-permute-done.11), channel_id=1, source_target_pairs={{2,0},{4,2},{6,4},{8,6},{10,8},{12,10},{14,12},{16,14},{18,16},{20... | collective-permute-start | bytes 3145736 | tf_op jit(solution)/shard_map/ppermute | solution.py:29
  692.4 73.1 %copy-start.32 = (bf16[128,4096]{1,0:T(8,128)(2,1)}, bf16[128,4096]{1,0:T(8,128)(2,1)S(1)}, u32[]{:S(2)}) copy-start(bf16[128,4096]{1,0:T(8,128)(2,1)S(1)} %collective-permute-done.5) | copy-start | bytes 3145732
  692.4 73.1 %collective-permute-start.6 = (bf16[128,4096]{1,0:T(8,128)(2,1)S(1)}, bf16[128,4096]{1,0:T(8,128)(2,1)}, u32[]{:S(2)}, u32[]{:S(2)}) collective-permute-start(bf16[128,4096]{1,0:T(8,128)(2,1)S(1)} %collective-permute-done.5), channel_id=1, source_target_pairs={{0,2},{2,4},{4,6},{6,8},{8,10},{10,12},{12,14},{14,16},{16,18},{18... | collective-permute-start | bytes 3145736 | tf_op jit(solution)/shard_map/ppermute | solution.py:27
  732.4 140.2 %collective-permute-start.13 = (bf16[128,4096]{1,0:T(8,128)(2,1)}, bf16[128,4096]{1,0:T(8,128)(2,1)}, u32[]{:S(2)}, u32[]{:S(2)}) collective-permute-start(bf16[128,4096]{1,0:T(8,128)(2,1)} %collective-permute-done.12), channel_id=1, source_target_pairs={{2,0},{4,2},{6,4},{8,6},{10,8},{12,10},{14,12},{16,14},{18,16},{20... | collective-permute-start | bytes 3145736 | tf_op jit(solution)/shard_map/ppermute | solution.py:29
  765.5 112.7 %collective-permute-start.7 = (bf16[128,4096]{1,0:T(8,128)(2,1)}, bf16[128,4096]{1,0:T(8,128)(2,1)}, u32[]{:S(2)}, u32[]{:S(2)}) collective-permute-start(bf16[128,4096]{1,0:T(8,128)(2,1)} %collective-permute-done.6), channel_id=1, source_target_pairs={{0,2},{2,4},{4,6},{6,8},{8,10},{10,12},{12,14},{14,16},{16,18},{18... | collective-permute-start | bytes 3145736 | tf_op jit(solution)/shard_map/ppermute | solution.py:27
  872.6 70.6 %collective-permute-start.14 = (bf16[128,4096]{1,0:T(8,128)(2,1)}, bf16[128,4096]{1,0:T(8,128)(2,1)S(1)}, u32[]{:S(2)}, u32[]{:S(2)}) collective-permute-start(bf16[128,4096]{1,0:T(8,128)(2,1)} %collective-permute-done.13), channel_id=1, source_target_pairs={{2,0},{4,2},{6,4},{8,6},{10,8},{12,10},{14,12},{16,14},{18,16},{20... | collective-permute-start | bytes 3145736 | tf_op jit(solution)/shard_map/ppermute | solution.py:29
  1031.5 133.3 %copy-start.9 = (bf16[1,256,2048]{2,1,0:T(8,128)(2,1)S(1)}, bf16[1,256,2048]{2,1,0:T(8,128)(2,1)}, u32[]{:S(2)}) copy-start(bf16[1,256,2048]{2,1,0:T(8,128)(2,1)} %param.23) | copy-start | bytes 3145732
  1164.8 85.4 %reduce-scatter.8.cloned.1.call-start = ((), (), s32[]{:S(2)}) async-start(), calls=%async_computation.16 | async-start | bytes 655360 | tf_op jit(solution)/shard_map/reduce_scatter | solution.py:256
  1199.8 15.6 slice-start.1
  1199.8 15.6 slice-start.2
  1199.8 15.6 slice-start.3
  1229.8 42.5 %reduce-scatter.10.cloned.1.call-start = ((), (), s32[]{:S(2)}) async-start(), calls=%async_computation.17 | async-start | bytes 655360 | tf_op jit(solution)/shard_map/reduce_scatter | solution.py:259
  1240.5 122.9 %all-reduce.12.cloned.1.call-start = ((), (), s32[]{:S(2)}) async-start(), calls=%async_computation.23 | async-start | bytes 4194304 | tf_op jit(solution)/shard_map/psum | solution.py:192
  1275.7 2109.4 %reduce-scatter.20.cloned.1.call-start = ((), (), s32[]{:S(2)}) async-start(), calls=%async_computation.22 | async-start | bytes 106954752 | tf_op jit(solution)/shard_map/reduce_scatter | solution.py:224
  1342.7 2129.9 %reduce-scatter.16.cloned.1.call-start = ((), (), s32[]{:S(2)}) async-start(), calls=%async_computation.20 | async-start | bytes 2228224 | tf_op jit(solution)/shard_map/reduce_scatter | solution.py:285
  1345.8 2210.5 %reduce-scatter.14.cloned.1.call-start = ((), (), s32[]{:S(2)}) async-start(), calls=%async_computation.19 | async-start | bytes 2228224 | tf_op jit(solution)/shard_map/reduce_scatter | solution.py:284
  1347.8 2390.0 %reduce-scatter.18.cloned.1.call-start = ((), (), s32[]{:S(2)}) async-start(), calls=%async_computation.21 | async-start | bytes 8912896 | tf_op jit(solution)/shard_map/reduce_scatter | solution.py:286
  1354.2 2566.1 %reduce-scatter.12.cloned.1.call-start = ((), (), s32[]{:S(2)}) async-start(), calls=%async_computation.18 | async-start | bytes 8912896 | tf_op jit(solution)/shard_map/reduce_scatter | solution.py:283
  1361.5 83.9 %copy-start.42 = (f32[256]{0:T(256)S(1)}, f32[256]{0:T(256)}, u32[]{:S(2)}) copy-start(f32[256]{0:T(256)} %get-tuple-element.96) | copy-start | bytes 3076
  (36 other events, 211.9 us)
Sparse Core Ops, SparseCore 0:
  11.3 58.0 all-gather.13
  72.8 54.1 all-gather.11
  130.3 75.9 all-gather.15
  209.4 74.4 all-gather.17
  288.9 19.7 all-reduce.7
  312.3 355.1 all-gather.21
  671.2 285.3 all-gather.19
  959.7 192.5 all-gather.23
  1164.9 17.7 all-reduce.9
  1229.9 20.1 reduce-scatter.7
  1252.4 19.8 reduce-scatter.9
  1275.9 19.5 all-reduce.11
  1342.8 2042.2 reduce-scatter.19
  3387.8 84.7 reduce-scatter.15
  3475.3 80.9 reduce-scatter.13
  3559.0 178.7 reduce-scatter.17
  3740.5 179.8 reduce-scatter.11
